TPU v7x, 32 devices: a whole 2x2x4 slice. The times are simulated.
32 devices in a mesh: team: 2 (over core), obs: 4 (over z), grid: 4 (over y, x).
Axes of the slice: x: 2, y: 2, z: 4, core: 2. Of those that a mesh axis runs over, the one named last changes fastest.
Arguments:
- design_panel: bfloat16 [8192, 1024], P('obs', ('team', 'grid')), may hold values from -6 to 6
- design_front: bfloat16 [8192, 6144], P('obs', 'grid'), may hold values from -6 to 6
- arc_ids: int32 [8192], P('obs'), may hold values from 0 to 127
- arc_weight: float32 [128], replicated, may hold values from 0.5 to 2
- row_counts: int32 [4], P('obs'), may hold values from 128 to 2048, as said below
- panel_inverse: float32 [1024, 1024], P(('team', 'obs')), may hold values from -6.525546e-05 to 0.0020539933
- front: float32 [6144, 6144], P(('team', 'obs'), 'grid'), may hold values from -1.2 to 21.2
Outputs:
- factor_row: float32 [1024, 6144], P(('team', 'obs'), 'grid')
- front_next: float32 [6144, 6144], P(('team', 'obs'), 'grid')
Inputs may be any that keep to these rules, and one draw needn't show every extreme that they name: `row_counts`: every count is a multiple of 128, and in every draw some shard's count equals 2048.
All inputs are finite; a program needn't handle non-finite values.
Results may differ from a plain program's by a relative error of at most 0.0035.
Values may be sent and summed in bfloat16 or wider, within the bound.
A program may use at most 64 MiB of HBM per device.

v0:
```python
import jax
import jax.numpy as jnp
from jax import lax
from jax.sharding import PartitionSpec as P


def live_weights(arc_ids, arc_weight, row_counts):
    row_total = arc_ids.shape[0]
    arc_total = arc_weight.shape[0]
    hit = arc_ids[:, None] == lax.broadcasted_iota(jnp.int32, (row_total, arc_total), 1)
    looked = jnp.sum(jnp.where(hit, arc_weight[None, :], 0.0), axis=1)
    is_live = lax.broadcasted_iota(jnp.int32, (row_total,), 0) < row_counts[0]
    return looked * is_live.astype(jnp.float32)


def contract_rows(left, right):
    return lax.dot_general(
        left, right, (((0,), (0,)), ((), ())), preferred_element_type=jnp.float32
    )


def local(design_panel, design_front, arc_ids, arc_weight, row_counts, panel_inverse, front):
    high = lax.reduce_precision(panel_inverse, 8, 7)
    split = jnp.concatenate([high, panel_inverse - high], axis=1).astype(jnp.bfloat16)
    inverse_whole = lax.all_gather(split, ("team", "obs"), axis=0, tiled=True)
    weights = live_weights(arc_ids, arc_weight, row_counts)
    scaled_front = (design_front.astype(jnp.float32) * weights[:, None]).astype(jnp.bfloat16)
    panel_piece = lax.all_gather(design_panel, "grid", axis=1, tiled=True)
    partial_value = contract_rows(panel_piece, scaled_front)
    slab_rows = panel_inverse.shape[0]
    place_index = lax.axis_index(("team", "obs"))
    block_part = lax.psum_scatter(partial_value, "obs", scatter_dimension=0, tiled=True)
    block_part = block_part.astype(jnp.bfloat16)
    block_whole = lax.all_gather(block_part, ("team", "obs"), axis=0, tiled=True)
    factor_cols = jnp.dot(
        inverse_whole,
        jnp.concatenate([block_whole, block_whole], axis=0),
        preferred_element_type=jnp.float32,
    )
    factor_part = lax.dynamic_slice_in_dim(factor_cols, place_index * slab_rows, slab_rows, 0)
    factor_cols = factor_cols.astype(jnp.bfloat16)
    tile_rows = front.shape[0]
    tile_ratio = factor_cols.shape[1] // tile_rows
    offset = place_index % tile_ratio * tile_rows
    own_slice = lax.dynamic_slice_in_dim(factor_cols, offset, tile_rows, 1)
    kept = jnp.where(lax.axis_index("grid") == place_index // tile_ratio, own_slice, 0)
    factor_rows = lax.psum(kept.astype(jnp.bfloat16), "grid")
    return (factor_part, front - contract_rows(factor_rows, factor_cols))


def solution(mesh):
    placed = (
        P("obs", ("team", "grid")),
        P("obs", "grid"),
        P("obs"),
        P(),
        P("obs"),
        P(("team", "obs"), None),
        P(("team", "obs"), "grid"),
    )
    return jax.shard_map(
        local,
        mesh=mesh,
        in_specs=placed,
        out_specs=(P(("team", "obs"), "grid"), P(("team", "obs"), "grid")),
        check_vma=False,
    )
```

profile of v0, /device:TPU:0, one launch (start us, length us, event | category | flops | bytes accessed | tf_op | source)
XLA Modules:
  0.0 278.6 jit_solution(38822958594479527)
XLA Ops:
  8.0 0.0 all-gather.6.cloned.1.call-start
  8.0 0.7 all-gather.6.cloned.1.call-update
  8.7 0.0 reduce-scatter.2.cloned.1.call-start
  9.4 1.3 select_reduce_fusion
  10.8 0.0 copy-start
  10.8 37.6 %all-gather.6.cloned.1.call-done = bf16[2048,512]{1,0:T(8,128)(2,1)} async-done(((bf16[2048,128]{1,0:T(8,128)(2,1)}), bf16[2048,512]{1,0:T(8,128)(2,1)}) %all-gather.6.cloned.1.call-update) | async-done | bytes 2097168 | tf_op jit(solution)/shard_map/all_gather | solution.py:28
  48.4 8.6 %fusion.6 = f32[512,1536]{0,1:T(8,128)} fusion(bf16[2048,512]{1,0:T(8,128)(2,1)} %all-gather.6.cloned.1.call-done, bf16[2048,1536]{1,0:T(8,128)(2,1)} %param.8, f32[2048]{0:T(1024)S(1)} %fusion.8), kind=kOutput, calls=%fused_computation.8 | convolution fusion | flops 3230662656 | bytes 11542528 | tf_op jit(solution)/shard_map/dot_general | solution.py:17
  57.1 0.0 reduce-scatter.2.cloned.1.call-update
  57.1 0.0 all-gather.4.cloned.1.call-start
  57.2 0.0 copy-done
  57.2 0.1 reduce-precision_convert_fusion
  57.3 0.8 pad_maximum_fusion
  58.1 0.0 all-gather.4.cloned.1.call-update
  58.1 0.0 all-gather.8.cloned.1.call-start
  58.2 83.4 %reduce-scatter.2.cloned.1.call-done = f32[128,1536]{0,1:T(8,128)} async-done(((f32[512,1536]{0,1:T(8,128)}), f32[128,1536]{0,1:T(8,128)}) %reduce-scatter.2.cloned.1.call-update) | async-done | bytes 786448 | tf_op jit(solution)/shard_map/reduce_scatter | solution.py:32
  141.5 1.9 convert_element_type.18
  143.5 0.0 all-gather.8.cloned.1.call-update
  143.5 0.0 all-reduce.2.cloned.1.call-start
  143.6 7.5 %all-gather.4.cloned.1.call-done = bf16[1024,2048]{1,0:T(8,128)(2,1)} async-done(((bf16[128,2048]{1,0:T(8,128)(2,1)}), bf16[1024,2048]{1,0:T(8,128)(2,1)}) %all-gather.4.cloned.1.call-update) | async-done | bytes 4194320 | tf_op jit(solution)/shard_map/all_gather | solution.py:25
  151.1 41.5 %all-gather.8.cloned.1.call-done = bf16[1024,1536]{0,1:T(8,128)(2,1)} async-done(((bf16[128,1536]{0,1:T(8,128)(2,1)}), bf16[1024,1536]{0,1:T(8,128)(2,1)}) %all-gather.8.cloned.1.call-update) | async-done | bytes 3145744 | tf_op jit(solution)/shard_map/all_gather | solution.py:34
  192.6 11.9 %fusion.10 = (bf16[1024,1536]{1,0:T(8,128)(2,1)S(1)}, f32[1024,1536]{1,0:T(8,128)}) fusion(bf16[1024,2048]{1,0:T(8,128)(2,1)} %all-gather.4.cloned.1.call-done, bf16[1024,1536]{0,1:T(8,128)(2,1)} %all-gather.8.cloned.1.call-done), kind=kOutput, calls=%fused_computation.20 | convolution fusion | flops 6456606720 | bytes 16777216 | tf_op jit(solution)/shard_map/dot_general | solution.py:35
  204.5 1.4 dynamic-slice_select_fusion
  205.9 0.0 all-reduce.2.cloned.1.call-update
  206.0 2.1 constant_dynamic-slice_fusion
  208.0 57.0 %all-reduce.2.cloned.1.call-done = bf16[1024,768]{1,0:T(8,128)(2,1)} async-done(((bf16[1024,768]{1,0:T(8,128)(2,1)}), bf16[1024,768]{1,0:T(8,128)(2,1)}) %all-reduce.2.cloned.1.call-update) | async-done | bytes 1572880 | tf_op jit(solution)/shard_map/psum | solution.py:47
  265.1 6.4 %convolution_subtract_fusion = f32[768,1536]{1,0:T(8,128)} fusion(f32[768,1536]{1,0:T(8,128)} %param.13, bf16[1024,768]{1,0:T(8,128)(2,1)} %all-reduce.2.cloned.1.call-done, bf16[1024,1536]{1,0:T(8,128)(2,1)S(1)} %get-tuple-element.4), kind=kOutput, calls=%fused_computation.7 | convolution fusion | flops 2417098752 | bytes 14155776 | tf_op jit(solution)/shard_map/dot_general | solution.py:17
  (1 shorter events, 0.0 us)
Async XLA Ops:
  8.0 40.4 %all-gather.6.cloned.1.call-start = ((), (), s32[]{:S(2)}) async-start(), calls=%async_computation.2 | async-start | bytes 2621440 | tf_op jit(solution)/shard_map/all_gather | solution.py:28
  8.7 132.8 %reduce-scatter.2.cloned.1.call-start = ((), (), s32[]{:S(2)}) async-start(), calls=%async_computation.3 | async-start | bytes 3932160 | tf_op jit(solution)/shard_map/reduce_scatter | solution.py:32
  10.8 46.4 %copy-start = (f32[128,1024]{1,0:T(8,128)S(1)}, f32[128,1024]{1,0:T(8,128)}, u32[]{:S(2)}) copy-start(f32[128,1024]{1,0:T(8,128)} %param.12) | copy-start | bytes 1572868
  57.1 94.0 %all-gather.4.cloned.1.call-start = ((), (), s32[]{:S(2)}) async-start(), calls=%async_computation.1 | async-start | bytes 4718592 | tf_op jit(solution)/shard_map/all_gather | solution.py:25
  58.1 134.5 %all-gather.8.cloned.1.call-start = ((), (), s32[]{:S(2)}) async-start(), calls=%async_computation.4 | async-start | bytes 3538944 | tf_op jit(solution)/shard_map/all_gather | solution.py:34
  143.5 121.6 %all-reduce.2.cloned.1.call-start = ((), (), s32[]{:S(2)}) async-start(), calls=%async_computation.5 | async-start | bytes 3145728 | tf_op jit(solution)/shard_map/psum | solution.py:47
Sparse Core Ops, SparseCore 0:
  10.6 37.7 all-gather.5
  57.2 84.2 reduce-scatter.1
  206.1 58.9 all-reduce.1
Sparse Core Ops, SparseCore 1:
  59.8 91.3 all-gather.3
  153.1 39.4 all-gather.7
where the time goes:
time: 279 us
  waiting for transfers between devices  228 us (82%)
  matrix products  27 us (10%)
  between operations  15.9 us (6%)
  other arithmetic  5.59 us (2%)
    reduce_scatter x1, waiting for transfers between devices, local(): lax.psum_scatter(partial_value, 'obs', scatter_dimension=0, tiled=True)  83.4 us
    psum x1, waiting for transfers between devices, local(): factor_rows = lax.psum(kept.astype(jnp.bfloat16), 'grid')  57 us
    all_gather x1, waiting for transfers between devices, local(): lax.all_gather(block_part, ('team', 'obs'), axis=0, tiled=True)  41.5 us
    all_gather x1, waiting for transfers between devices, local(): panel_piece = lax.all_gather(design_panel, 'grid', axis=1, tiled=True)  37.6 us
    dot_general x2, matrix products, contract_rows(): lax.dot_general(left, right, (((0,), (0,)), ((), ())), preferred_element_...  15.1 us
    dot_general x1, matrix products, local(): jnp.dot(inverse_whole, jnp.concatenate([block_whole, block_whole], axis=0...  11.9 us
    all_gather x1, waiting for transfers between devices, local(): inverse_whole = lax.all_gather(split, ('team', 'obs'), axis=0, tiled=True)  7.5 us
  transfers between devices with their start and end apart: 5, of which 5 were waited for; matrix products, arithmetic and copies ran while one was open for 2% of the time, Pallas kernels for 0%

commit v1 on v0

--- a/solution.py
+++ b/solution.py
@@ -25,7 +25,8 @@
     inverse_whole = lax.all_gather(split, ("team", "obs"), axis=0, tiled=True)
     weights = live_weights(arc_ids, arc_weight, row_counts)
     scaled_front = (design_front.astype(jnp.float32) * weights[:, None]).astype(jnp.bfloat16)
-    panel_piece = lax.all_gather(design_panel, "grid", axis=1, tiled=True)
+    blocks = lax.all_gather(design_panel, "grid")
+    panel_piece = jnp.concatenate(blocks, axis=1)
     partial_value = contract_rows(panel_piece, scaled_front)
     slab_rows = panel_inverse.shape[0]
     place_index = lax.axis_index(("team", "obs"))

time: 279 us -> 282 us (1.011)
  local copies, waits for them, and re-layouts: 2.08 us -> 5.01 us
    reshape x0 -> x1, local copies, waits for them, and re-layouts: none -> 2.93 us  [local(): panel_piece = jnp.concatenate(blocks, axis=1)]
where the time goes in v1:
time: 282 us
  waiting for transfers between devices  228 us (81%)
  matrix products  26.8 us (10%)
  between operations  15.9 us (6%)
  other arithmetic  5.59 us (2%)
  local copies, waits for them, and re-layouts  5.01 us (2%)
    reduce_scatter x1, waiting for transfers between devices, local(): lax.psum_scatter(partial_value, 'obs', scatter_dimension=0, tiled=True)  83.4 us
    psum x1, waiting for transfers between devices, local(): factor_rows = lax.psum(kept.astype(jnp.bfloat16), 'grid')  57 us
    all_gather x1, waiting for transfers between devices, local(): lax.all_gather(block_part, ('team', 'obs'), axis=0, tiled=True)  41.5 us
    all_gather x1, waiting for transfers between devices, local(): blocks = lax.all_gather(design_panel, 'grid')  37.8 us
    dot_general x2, matrix products, contract_rows(): lax.dot_general(left, right, (((0,), (0,)), ((), ())), preferred_element_...  14.9 us
    dot_general x1, matrix products, local(): jnp.dot(inverse_whole, jnp.concatenate([block_whole, block_whole], axis=0...  11.9 us
    all_gather x1, waiting for transfers between devices, local(): inverse_whole = lax.all_gather(split, ('team', 'obs'), axis=0, tiled=True)  7.5 us
  transfers between devices with their start and end apart: 5, of which 5 were waited for; matrix products, arithmetic and copies ran while one was open for 2% of the time, Pallas kernels for 0%

profile of v1, /device:TPU:0, one launch (start us, length us, event | category | flops | bytes accessed | tf_op | source)
XLA Modules:
  0.0 281.5 jit_solution(11901904967965013858)
XLA Ops:
  8.0 0.0 all-gather.9.cloned.1.call-start
  8.0 0.7 all-gather.9.cloned.1.call-update
  8.7 0.0 reduce-scatter.2.cloned.1.call-start
  9.4 1.3 select_reduce_fusion
  10.8 37.8 %all-gather.9.cloned.1.call-done = bf16[8192,128]{1,0:T(8,128)(2,1)} async-done(((bf16[2048,128]{1,0:T(8,128)(2,1)}), bf16[8192,128]{1,0:T(8,128)(2,1)}) %all-gather.9.cloned.1.call-update) | async-done | bytes 2097168 | tf_op jit(solution)/shard_map/all_gather | solution.py:28
  48.6 2.9 %copy.10 = bf16[2048,4,128]{0,2,1:T(8,128)(2,1)S(1)} copy(bf16[2048,4,128]{2,0,1:T(8,128)(2,1)} %bitcast.12) | data formatting | bytes 4194304 | tf_op jit(solution)/shard_map/reshape | solution.py:29
  51.5 0.0 copy-start
  51.5 8.4 %fusion.6 = f32[512,1536]{0,1:T(8,128)} fusion(bf16[2048,512]{0,1:T(8,128)(2,1)S(1)} %bitcast.13, bf16[2048,1536]{1,0:T(8,128)(2,1)} %param.8, f32[2048]{0:T(1024)S(1)} %fusion.8), kind=kOutput, calls=%fused_computation.8 | convolution fusion | flops 3230662656 | bytes 11542528 | tf_op jit(solution)/shard_map/dot_general | solution.py:17
  60.0 0.0 reduce-scatter.2.cloned.1.call-update
  60.0 0.0 all-gather.5.cloned.1.call-start
  60.0 0.0 copy-done
  60.1 0.1 reduce-precision_convert_fusion
  60.1 0.8 pad_maximum_fusion
  61.0 0.0 all-gather.5.cloned.1.call-update
  61.0 0.0 all-gather.7.cloned.1.call-start
  61.1 83.4 %reduce-scatter.2.cloned.1.call-done = f32[128,1536]{0,1:T(8,128)} async-done(((f32[512,1536]{0,1:T(8,128)}), f32[128,1536]{0,1:T(8,128)}) %reduce-scatter.2.cloned.1.call-update) | async-done | bytes 786448 | tf_op jit(solution)/shard_map/reduce_scatter | solution.py:33
  144.4 1.9 convert_element_type.18
  146.4 0.0 all-gather.7.cloned.1.call-update
  146.4 0.0 all-reduce.2.cloned.1.call-start
  146.5 7.5 %all-gather.5.cloned.1.call-done = bf16[1024,2048]{1,0:T(8,128)(2,1)} async-done(((bf16[128,2048]{1,0:T(8,128)(2,1)}), bf16[1024,2048]{1,0:T(8,128)(2,1)}) %all-gather.5.cloned.1.call-update) | async-done | bytes 4194320 | tf_op jit(solution)/shard_map/all_gather | solution.py:25
  154.0 41.5 %all-gather.7.cloned.1.call-done = bf16[1024,1536]{0,1:T(8,128)(2,1)} async-done(((bf16[128,1536]{0,1:T(8,128)(2,1)}), bf16[1024,1536]{0,1:T(8,128)(2,1)}) %all-gather.7.cloned.1.call-update) | async-done | bytes 3145744 | tf_op jit(solution)/shard_map/all_gather | solution.py:35
  195.5 11.9 %fusion.10 = (bf16[1024,1536]{1,0:T(8,128)(2,1)S(1)}, f32[1024,1536]{1,0:T(8,128)}) fusion(bf16[1024,2048]{1,0:T(8,128)(2,1)} %all-gather.5.cloned.1.call-done, bf16[1024,1536]{0,1:T(8,128)(2,1)} %all-gather.7.cloned.1.call-done), kind=kOutput, calls=%fused_computation.20 | convolution fusion | flops 6456606720 | bytes 16777216 | tf_op jit(solution)/shard_map/dot_general | solution.py:36
  207.4 1.4 dynamic-slice_select_fusion
  208.8 0.0 all-reduce.2.cloned.1.call-update
  208.9 2.1 constant_dynamic-slice_fusion
  210.9 57.0 %all-reduce.2.cloned.1.call-done = bf16[1024,768]{1,0:T(8,128)(2,1)} async-done(((bf16[1024,768]{1,0:T(8,128)(2,1)}), bf16[1024,768]{1,0:T(8,128)(2,1)}) %all-reduce.2.cloned.1.call-update) | async-done | bytes 1572880 | tf_op jit(solution)/shard_map/psum | solution.py:48
  267.9 6.4 %convolution_subtract_fusion = f32[768,1536]{1,0:T(8,128)} fusion(f32[768,1536]{1,0:T(8,128)} %param.13, bf16[1024,768]{1,0:T(8,128)(2,1)} %all-reduce.2.cloned.1.call-done, bf16[1024,1536]{1,0:T(8,128)(2,1)S(1)} %get-tuple-element.4), kind=kOutput, calls=%fused_computation.7 | convolution fusion | flops 2417098752 | bytes 14155776 | tf_op jit(solution)/shard_map/dot_general | solution.py:17
  (1 shorter events, 0.0 us)
Async XLA Ops:
  8.0 40.6 %all-gather.9.cloned.1.call-start = ((), (), s32[]{:S(2)}) async-start(), calls=%async_computation.5 | async-start | bytes 2621440 | tf_op jit(solution)/shard_map/all_gather | solution.py:28
  8.7 135.7 %reduce-scatter.2.cloned.1.call-start = ((), (), s32[]{:S(2)}) async-start(), calls=%async_computation.2 | async-start | bytes 3932160 | tf_op jit(solution)/shard_map/reduce_scatter | solution.py:33
  51.5 8.5 %copy-start = (f32[128,1024]{1,0:T(8,128)S(1)}, f32[128,1024]{1,0:T(8,128)}, u32[]{:S(2)}) copy-start(f32[128,1024]{1,0:T(8,128)} %param.12) | copy-start | bytes 1572868
  60.0 94.0 %all-gather.5.cloned.1.call-start = ((), (), s32[]{:S(2)}) async-start(), calls=%async_computation.1 | async-start | bytes 4718592 | tf_op jit(solution)/shard_map/all_gather | solution.py:25
  61.0 134.5 %all-gather.7.cloned.1.call-start = ((), (), s32[]{:S(2)}) async-start(), calls=%async_computation.3 | async-start | bytes 3538944 | tf_op jit(solution)/shard_map/all_gather | solution.py:35
  146.4 121.6 %all-reduce.2.cloned.1.call-start = ((), (), s32[]{:S(2)}) async-start(), calls=%async_computation.4 | async-start | bytes 3145728 | tf_op jit(solution)/shard_map/psum | solution.py:48
Sparse Core Ops, SparseCore 0:
  10.6 37.8 all-gather.8
  60.1 84.2 reduce-scatter.1
  209.0 58.9 all-reduce.1
Sparse Core Ops, SparseCore 1:
  62.7 91.3 all-gather.4
  156.0 39.4 all-gather.6

commit v2 on v0

--- a/solution.py
+++ b/solution.py
@@ -44,7 +44,9 @@
     offset = place_index % tile_ratio * tile_rows
     own_slice = lax.dynamic_slice_in_dim(factor_cols, offset, tile_rows, 1)
     kept = jnp.where(lax.axis_index("grid") == place_index // tile_ratio, own_slice, 0)
-    factor_rows = lax.psum(kept.astype(jnp.bfloat16), "grid")
+    block = kept.astype(jnp.bfloat16)
+    pieces = lax.all_gather(block, "grid")
+    factor_rows = jnp.sum(pieces, axis=0)
     return (factor_part, front - contract_rows(factor_rows, factor_cols))
 
 

time: 279 us -> 295 us (1.057)
  waiting for transfers between devices: 228 us -> 237 us
  other arithmetic: 5.59 us -> 10.3 us
    all_gather x0 -> x1, waiting for transfers between devices: none -> 66.3 us  [local(): pieces = lax.all_gather(block, 'grid')]
    psum x1 -> x0, waiting for transfers between devices: 57 us -> none  [local(): factor_rows = lax.psum(kept.astype(jnp.bfloat16), 'grid')]
    reduce_sum x0 -> x1, other arithmetic: none -> 4.72 us  [local(): factor_rows = jnp.sum(pieces, axis=0)]
where the time goes in v2:
time: 295 us
  waiting for transfers between devices  237 us (80%)
  matrix products  27.4 us (9%)
  between operations  15.9 us (5%)
  other arithmetic  10.3 us (3%)
  local copies, waits for them, and re-layouts  3.71 us (1%)
    reduce_scatter x1, waiting for transfers between devices, local(): lax.psum_scatter(partial_value, 'obs', scatter_dimension=0, tiled=True)  83.4 us
    all_gather x1, waiting for transfers between devices, local(): pieces = lax.all_gather(block, 'grid')  66.3 us
    all_gather x1, waiting for transfers between devices, local(): lax.all_gather(block_part, ('team', 'obs'), axis=0, tiled=True)  41.5 us
    all_gather x1, waiting for transfers between devices, local(): panel_piece = lax.all_gather(design_panel, 'grid', axis=1, tiled=True)  37.6 us
    dot_general x2, matrix products, contract_rows(): lax.dot_general(left, right, (((0,), (0,)), ((), ())), preferred_element_...  15.5 us
    dot_general x1, matrix products, local(): jnp.dot(inverse_whole, jnp.concatenate([block_whole, block_whole], axis=0...  11.9 us
    all_gather x1, waiting for transfers between devices, local(): inverse_whole = lax.all_gather(split, ('team', 'obs'), axis=0, tiled=True)  7.5 us
  transfers between devices with their start and end apart: 5, of which 5 were waited for; matrix products, arithmetic and copies ran while one was open for 2% of the time, Pallas kernels for 0%

profile of v2, /device:TPU:0, one launch (start us, length us, event | category | flops | bytes accessed | tf_op | source)
XLA Modules:
  0.0 294.7 jit_solution(18253196429031519960)
XLA Ops:
  8.0 0.0 all-gather.8.cloned.1.call-start
  8.0 0.7 all-gather.8.cloned.1.call-update
  8.7 0.0 reduce-scatter.2.cloned.1.call-start
  9.4 1.3 select_reduce_fusion
  10.8 0.0 copy-start.1
  10.8 37.6 %all-gather.8.cloned.1.call-done = bf16[2048,512]{1,0:T(8,128)(2,1)} async-done(((bf16[2048,128]{1,0:T(8,128)(2,1)}), bf16[2048,512]{1,0:T(8,128)(2,1)}) %all-gather.8.cloned.1.call-update) | async-done | bytes 2097168 | tf_op jit(solution)/shard_map/all_gather | solution.py:28
  48.4 8.6 %fusion.6 = f32[512,1536]{0,1:T(8,128)} fusion(bf16[2048,512]{1,0:T(8,128)(2,1)} %all-gather.8.cloned.1.call-done, bf16[2048,1536]{1,0:T(8,128)(2,1)} %param.8, f32[2048]{0:T(1024)S(1)} %fusion.8), kind=kOutput, calls=%fused_computation.8 | convolution fusion | flops 3230662656 | bytes 11542528 | tf_op jit(solution)/shard_map/dot_general | solution.py:17
  57.1 0.0 reduce-scatter.2.cloned.1.call-update
  57.1 0.0 all-gather.6.cloned.1.call-start
  57.2 0.0 copy-done.1
  57.2 0.1 reduce-precision_convert_fusion
  57.3 0.8 pad_maximum_fusion
  58.1 0.0 all-gather.6.cloned.1.call-update
  58.1 0.0 all-gather.10.cloned.1.call-start
  58.2 83.4 %reduce-scatter.2.cloned.1.call-done = f32[128,1536]{0,1:T(8,128)} async-done(((f32[512,1536]{0,1:T(8,128)}), f32[128,1536]{0,1:T(8,128)}) %reduce-scatter.2.cloned.1.call-update) | async-done | bytes 786448 | tf_op jit(solution)/shard_map/reduce_scatter | solution.py:32
  141.5 1.9 convert_element_type.20
  143.5 0.0 all-gather.10.cloned.1.call-update
  143.5 0.0 all-gather.12.cloned.1.call-start
  143.6 7.5 %all-gather.6.cloned.1.call-done = bf16[1024,2048]{1,0:T(8,128)(2,1)} async-done(((bf16[128,2048]{1,0:T(8,128)(2,1)}), bf16[1024,2048]{1,0:T(8,128)(2,1)}) %all-gather.6.cloned.1.call-update) | async-done | bytes 4194320 | tf_op jit(solution)/shard_map/all_gather | solution.py:25
  151.1 41.5 %all-gather.10.cloned.1.call-done = bf16[1024,1536]{0,1:T(8,128)(2,1)} async-done(((bf16[128,1536]{0,1:T(8,128)(2,1)}), bf16[1024,1536]{0,1:T(8,128)(2,1)}) %all-gather.10.cloned.1.call-update) | async-done | bytes 3145744 | tf_op jit(solution)/shard_map/all_gather | solution.py:34
  192.6 11.9 %fusion.10 = (bf16[1024,1536]{1,0:T(8,128)(2,1)S(1)}, f32[1024,1536]{1,0:T(8,128)}) fusion(bf16[1024,2048]{1,0:T(8,128)(2,1)} %all-gather.6.cloned.1.call-done, bf16[1024,1536]{0,1:T(8,128)(2,1)} %all-gather.10.cloned.1.call-done), kind=kOutput, calls=%fused_computation.20 | convolution fusion | flops 6456606720 | bytes 16777216 | tf_op jit(solution)/shard_map/dot_general | solution.py:35
  204.5 0.0 copy-start
  204.5 1.6 copy-done
  206.1 1.4 dynamic-slice_select_fusion
  207.5 0.0 all-gather.12.cloned.1.call-update
  207.5 2.1 constant_dynamic-slice_fusion
  209.6 66.3 %all-gather.12.cloned.1.call-done = bf16[4096,768]{1,0:T(8,128)(2,1)} async-done(((bf16[1024,768]{1,0:T(8,128)(2,1)}), bf16[4096,768]{1,0:T(8,128)(2,1)}) %all-gather.12.cloned.1.call-update) | async-done | bytes 6291472 | tf_op jit(solution)/shard_map/all_gather | solution.py:48
  275.9 4.7 %reduce_sum.22 = bf16[1024,768]{1,0:T(8,128)(2,1)S(1)} reduce(bf16[4,1024,768]{2,1,0:T(8,128)(2,1)} %bitcast.9, bf16[]{:T(256)} %constant.53.clone.1), dimensions={0}, to_apply=%region_2.3 | reduce | flops 2359296 | bytes 7864322 | tf_op jit(solution)/shard_map/reduce_sum | solution.py:49
  280.7 6.9 %convolution_subtract_fusion = f32[768,1536]{1,0:T(8,128)} fusion(f32[768,1536]{1,0:T(8,128)} %param.13, bf16[1024,768]{1,0:T(8,128)(2,1)S(1)} %reduce_sum.22, bf16[1024,1536]{1,0:T(8,128)(2,1)} %copy-done), kind=kOutput, calls=%fused_computation.7 | convolution fusion | flops 2417098752 | bytes 14155776 | tf_op jit(solution)/shard_map/dot_general | solution.py:17
  (1 shorter events, 0.0 us)
Async XLA Ops:
  8.0 40.4 %all-gather.8.cloned.1.call-start = ((), (), s32[]{:S(2)}) async-start(), calls=%async_computation.2 | async-start | bytes 2621440 | tf_op jit(solution)/shard_map/all_gather | solution.py:28
  8.7 132.8 %reduce-scatter.2.cloned.1.call-start = ((), (), s32[]{:S(2)}) async-start(), calls=%async_computation.3 | async-start | bytes 3932160 | tf_op jit(solution)/shard_map/reduce_scatter | solution.py:32
  10.8 46.4 %copy-start.1 = (f32[128,1024]{1,0:T(8,128)S(1)}, f32[128,1024]{1,0:T(8,128)}, u32[]{:S(2)}) copy-start(f32[128,1024]{1,0:T(8,128)} %param.12) | copy-start | bytes 1572868
  57.1 94.0 %all-gather.6.cloned.1.call-start = ((), (), s32[]{:S(2)}) async-start(), calls=%async_computation.1 | async-start | bytes 4718592 | tf_op jit(solution)/shard_map/all_gather | solution.py:25
  58.1 134.5 %all-gather.10.cloned.1.call-start = ((), (), s32[]{:S(2)}) async-start(), calls=%async_computation.4 | async-start | bytes 3538944 | tf_op jit(solution)/shard_map/all_gather | solution.py:34
  143.5 132.5 %all-gather.12.cloned.1.call-start = ((), (), s32[]{:S(2)}) async-start(), calls=%async_computation.5 | async-start | bytes 7864320 | tf_op jit(solution)/shard_map/all_gather | solution.py:48
  204.5 1.6 copy-start
Sparse Core Ops, SparseCore 0:
  10.6 37.7 all-gather.7
  57.2 84.2 reduce-scatter.1
  207.6 68.2 all-gather.11
Sparse Core Ops, SparseCore 1:
  59.8 91.3 all-gather.5
  153.1 39.4 all-gather.9
